TPU v7x, 32 devices: a whole 2x2x4 slice. The times are simulated.
32 devices in a mesh: dp: 2 (over x), ctx: 4 (over z), tp: 4 (over y, core).
Axes of the slice: x: 2, y: 2, z: 4, core: 2. Of those that a mesh axis runs over, the one named last changes fastest.
Arguments:
- hidden_in: bfloat16 [2, 2, 2048, 768], P(None, 'dp', 'ctx'), may hold values from -6 to 6
- prefix: int32 [2, 2], P(None, 'dp'), may hold values from 204 to 1024
- block_order: int32 [8], replicated, may hold values from 0 to 7, each once
- qkv_weight: bfloat16 [3, 768, 768], P(None, 'dp', 'tp'), may hold values from -0.3125 to 0.3125
- out_weight: bfloat16 [768, 768], P('tp', 'dp'), may hold values from -2.5 to 2.5
- up_weight: bfloat16 [768, 3072], P('dp', 'tp'), may hold values from -0.21875 to 0.21875
- down_weight: bfloat16 [3072, 768], P('tp', 'dp'), may hold values from -0.4375 to 0.4375
- ln_gains: bfloat16 [2, 768], P(None, 'dp'), may hold values from 0.5 to 1.5
- ln_shifts: bfloat16 [2, 768], P(None, 'dp'), may hold values from -2 to 2
- cotangent: bfloat16 [2, 2, 2048, 768], P(None, 'dp', 'ctx'), may hold values from -6 to 6
Outputs:
- block_out: bfloat16 [2, 2, 2048, 768], P(None, 'dp', 'ctx')
- grad_in: float32 [2, 2, 2048, 768], P(None, 'dp', 'ctx')
- grad_qkv: float32 [3, 768, 768], P(None, 'dp', 'tp')
- grad_out: float32 [768, 768], P('tp', 'dp')
- grad_up: float32 [768, 3072], P('dp', 'tp')
- grad_down: float32 [3072, 768], P('tp', 'dp')
- grad_gains: float32 [2, 768], P(None, 'dp')
- grad_shifts: float32 [2, 768], P(None, 'dp')
Inputs may be any that keep to these rules, and one draw needn't show every extreme that they name: `prefix`: leading positions of each sequence that all of its queries see. `block_order`: each of the 2 * 4 block numbers appears once.
All inputs are finite; a program needn't handle non-finite values.
Results may differ from a plain program's by a relative error of at most 0.012.
The roundings to bfloat16 on the way count: a program that leaves them out, or rounds other values in their place, can miss the bound.
Values may be sent and summed in bfloat16 or wider, within the bound.
A program may use at most 128 MiB of HBM per device.

v0:
```python
import jax
import jax.numpy as jnp
from jax import lax
from jax.sharding import PartitionSpec as P

HEAD_DIM = 64
DEPTH = 12
EPS = 1e-05
GELU_C = 0.7978845608028654
GELU_A = 0.044715
NEG = -1e30
ROW_BLOCK = 512


def apply_layer_norm(values, norm_gain, norm_shift):
    row_mean = jnp.mean(values, axis=1, keepdims=True)
    centered_input = values - row_mean
    inverse_deviation = lax.rsqrt(
        jnp.mean(centered_input * centered_input, axis=1, keepdims=True) + EPS
    )
    normalized_input = centered_input * inverse_deviation
    return (normalized_input * norm_gain + norm_shift, normalized_input, inverse_deviation)


def norm_backward(normed_gradient, normalized_input, inverse_deviation, norm_gain):
    scaled_gradient = normed_gradient * norm_gain
    return inverse_deviation * (
        scaled_gradient
        - jnp.mean(scaled_gradient, axis=1, keepdims=True)
        - normalized_input * jnp.mean(scaled_gradient * normalized_input, axis=1, keepdims=True)
    )


def gelu_value(u):
    return 0.5 * u * (1.0 + jnp.tanh(GELU_C * (u + GELU_A * u * u * u)))


def gelu_slope(u):
    inner = jnp.tanh(GELU_C * (u + GELU_A * u * u * u))
    return 0.5 * (1.0 + inner) + 0.5 * u * (1.0 - inner * inner) * GELU_C * (
        1.0 + 3.0 * GELU_A * u * u
    )


def block_positions(block_order, rows, half):
    slots = jnp.arange(block_order.shape[0], dtype=jnp.int32)
    picked = jnp.where((rows // half)[:, None] == slots[None, :], block_order[None, :], 0)
    return jnp.sum(picked, axis=1) * half + rows % half


def fetch_weights(qkv_weight, out_weight, up_weight, down_weight, ln_gains, ln_shifts):
    return (
        lax.all_gather(qkv_weight, "dp", axis=1, tiled=True),
        lax.all_gather(out_weight, "dp", axis=1, tiled=True),
        lax.all_gather(up_weight, "dp", axis=0, tiled=True),
        lax.all_gather(down_weight, "dp", axis=1, tiled=True),
        lax.all_gather(ln_gains, "dp", axis=1, tiled=True),
        lax.all_gather(ln_shifts, "dp", axis=1, tiled=True),
    )


def body(
    hidden_in,
    prefix,
    block_order,
    qkv_weight,
    out_weight,
    up_weight,
    down_weight,
    ln_gains,
    ln_shifts,
    cotangent,
):
    micro = hidden_in.shape[0]
    tokens = hidden_in.shape[2]
    width = hidden_in.shape[3]
    local_width = qkv_weight.shape[2]
    head_dim = HEAD_DIM
    local_heads = local_width // head_dim
    seq_len = tokens * lax.axis_size("ctx")
    half = tokens // 2
    branch = DEPTH ** (-0.5)
    scale = head_dim ** (-0.5)
    block_rows = min(tokens, ROW_BLOCK)
    blocks = tokens // block_rows
    query_rows = lax.axis_index("ctx") * tokens + jnp.arange(tokens, dtype=jnp.int32)
    key_rows = jnp.arange(seq_len, dtype=jnp.int32)
    query_pos = block_positions(block_order, query_rows, half)
    key_pos = block_positions(block_order, key_rows, half)
    acc_qkv = jnp.zeros((3, width, local_width), jnp.float32)
    acc_out = jnp.zeros((local_width, width), jnp.float32)
    acc_up = jnp.zeros((width, up_weight.shape[1]), jnp.float32)
    acc_down = jnp.zeros((down_weight.shape[0], width), jnp.float32)
    acc_gains = jnp.zeros((2, width), jnp.float32)
    acc_shifts = jnp.zeros((2, width), jnp.float32)
    results = []
    input_gradient_list = []
    for index in range(micro):
        full = fetch_weights(qkv_weight, out_weight, up_weight, down_weight, ln_gains, ln_shifts)
        qkv_full, out_full, up_full, down_full, gains_full, shifts_full = full
        norm_gains = gains_full.astype(jnp.float32)
        norm_shifts = shifts_full.astype(jnp.float32)
        input_rows = hidden_in[index, 0].astype(jnp.float32)
        allowed = (key_pos[None, :] <= query_pos[:, None]) | (key_pos[None, :] < prefix[index, 0])
        first_normed, normalized_first1, inverse_deviation1 = apply_layer_norm(
            input_rows, norm_gains[0], norm_shifts[0]
        )
        h1 = first_normed.astype(jnp.bfloat16)
        qkv = jnp.einsum("td,kde->kte", h1, qkv_full, preferred_element_type=jnp.float32).astype(
            jnp.bfloat16
        )
        keys_flat, values_flat = (
            lax.all_gather(qkv[1], "ctx", axis=0, tiled=True),
            lax.all_gather(qkv[2], "ctx", axis=0, tiled=True),
        )
        keys = keys_flat.reshape(seq_len, local_heads, head_dim)
        values = values_flat.reshape(seq_len, local_heads, head_dim)
        q_blocks = qkv[0].reshape(blocks, block_rows, local_heads, head_dim)
        a_blocks = allowed.reshape(blocks, block_rows, seq_len)

        def attend(item):
            q_blk, allow_blk = item
            scores = (
                jnp.einsum("qhd,khd->hqk", q_blk, keys, preferred_element_type=jnp.float32) * scale
            )
            scores = jnp.where(allow_blk[None], scores, NEG)
            top = jnp.max(scores, axis=2, keepdims=True)
            expd = jnp.exp(scores - top)
            total = jnp.sum(expd, axis=2, keepdims=True)
            prob = (expd / total).astype(jnp.bfloat16)
            mixed = jnp.einsum("hqk,khd->qhd", prob, values, preferred_element_type=jnp.float32)
            return (mixed.astype(jnp.bfloat16), (top + jnp.log(total))[:, :, 0])

        heads_out, logsum = lax.map(attend, (q_blocks, a_blocks))
        heads = heads_out.reshape(tokens, local_width)
        attn_part = jnp.dot(heads, out_full, preferred_element_type=jnp.float32)
        attn = lax.psum(attn_part, "tp")
        middle_state = input_rows + branch * attn
        second_normed, normalized_second2, inverse_deviation2 = apply_layer_norm(
            middle_state, norm_gains[1], norm_shifts[1]
        )
        h2 = second_normed.astype(jnp.bfloat16)
        up = jnp.dot(h2, up_full, preferred_element_type=jnp.float32)
        act = gelu_value(up).astype(jnp.bfloat16)
        mlp_part = jnp.dot(act, down_full, preferred_element_type=jnp.float32)
        mlp = lax.psum(mlp_part, "tp")
        results.append((middle_state + branch * mlp).astype(jnp.bfloat16))
        qkv_full, out_full, up_full, down_full, gains_full, shifts_full = fetch_weights(
            qkv_weight, out_weight, up_weight, down_weight, ln_gains, ln_shifts
        )
        upstream_gradient = cotangent[index, 0].astype(jnp.float32)
        d_mlp = (branch * upstream_gradient).astype(jnp.bfloat16)
        grad_down = jnp.einsum("tf,td->fd", act, d_mlp, preferred_element_type=jnp.float32)
        d_act = jnp.einsum("td,fd->tf", d_mlp, down_full, preferred_element_type=jnp.float32)
        d_up = (d_act * gelu_slope(up)).astype(jnp.bfloat16)
        grad_up = jnp.einsum("td,tf->df", h2, d_up, preferred_element_type=jnp.float32)
        n2_back = jnp.einsum("tf,df->td", d_up, up_full, preferred_element_type=jnp.float32)
        second_norm_gradient = lax.psum(n2_back, "tp")
        middle_gradient = upstream_gradient + norm_backward(
            second_norm_gradient, normalized_second2, inverse_deviation2, norm_gains[1]
        )
        d_attn = (branch * middle_gradient).astype(jnp.bfloat16)
        grad_out = jnp.einsum("te,td->ed", heads, d_attn, preferred_element_type=jnp.float32)
        d_heads = jnp.einsum(
            "td,ed->te", d_attn, out_full, preferred_element_type=jnp.float32
        ).astype(jnp.bfloat16)
        dh_blocks = d_heads.reshape(blocks, block_rows, local_heads, head_dim)

        def attend_back(carry, item):
            key_sum, value_sum = carry
            q_blk, allow_blk, lse_blk, dh_blk = item
            scores = (
                jnp.einsum("qhd,khd->hqk", q_blk, keys, preferred_element_type=jnp.float32) * scale
            )
            scores = jnp.where(allow_blk[None], scores, NEG)
            prob = jnp.exp(scores - lse_blk[:, :, None])
            prob_low = prob.astype(jnp.bfloat16)
            d_prob = jnp.einsum("qhd,khd->hqk", dh_blk, values, preferred_element_type=jnp.float32)
            d_scores = (prob * (d_prob - jnp.sum(prob * d_prob, axis=2, keepdims=True))).astype(
                jnp.bfloat16
            )
            d_query = (
                jnp.einsum("hqk,khd->qhd", d_scores, keys, preferred_element_type=jnp.float32)
                * scale
            ).astype(jnp.bfloat16)
            key_sum = (
                key_sum
                + jnp.einsum("hqk,qhd->khd", d_scores, q_blk, preferred_element_type=jnp.float32)
                * scale
            )
            value_sum = value_sum + jnp.einsum(
                "hqk,qhd->khd", prob_low, dh_blk, preferred_element_type=jnp.float32
            )
            return ((key_sum, value_sum), d_query)

        zero_kv = jnp.zeros((seq_len, local_heads, head_dim), jnp.float32)
        (key_sum, value_sum), d_query = lax.scan(
            attend_back, (zero_kv, zero_kv), (q_blocks, a_blocks, logsum, dh_blocks)
        )
        d_keys, d_values = (
            lax.psum_scatter(
                key_sum.reshape(seq_len, local_width), "ctx", scatter_dimension=0, tiled=True
            ),
            lax.psum_scatter(
                value_sum.reshape(seq_len, local_width), "ctx", scatter_dimension=0, tiled=True
            ),
        )
        d_qkv = jnp.stack(
            [
                d_query.reshape(tokens, local_width),
                d_keys.astype(jnp.bfloat16),
                d_values.astype(jnp.bfloat16),
            ]
        )
        grad_qkv = jnp.einsum("td,kte->kde", h1, d_qkv, preferred_element_type=jnp.float32)
        n1_back = jnp.einsum("kte,kde->td", d_qkv, qkv_full, preferred_element_type=jnp.float32)
        first_norm_gradient = lax.psum(n1_back, "tp")
        input_gradient_list.append(
            middle_gradient
            + norm_backward(
                first_norm_gradient, normalized_first1, inverse_deviation1, norm_gains[0]
            )
        )
        acc_gains = acc_gains + jnp.stack(
            [
                jnp.sum(first_norm_gradient * normalized_first1, axis=0),
                jnp.sum(second_norm_gradient * normalized_second2, axis=0),
            ]
        )
        acc_shifts = acc_shifts + jnp.stack(
            [jnp.sum(first_norm_gradient, axis=0), jnp.sum(second_norm_gradient, axis=0)]
        )
        acc_qkv = acc_qkv + grad_qkv
        acc_out = acc_out + grad_out
        acc_up = acc_up + grad_up
        acc_down = acc_down + grad_down
    whole_qkv, whole_out, whole_up, whole_down, whole_gains, whole_shifts = lax.psum(
        (acc_qkv, acc_out, acc_up, acc_down, acc_gains, acc_shifts), "ctx"
    )
    owned = (
        lax.psum_scatter(whole_qkv, "dp", scatter_dimension=1, tiled=True),
        lax.psum_scatter(whole_out, "dp", scatter_dimension=1, tiled=True),
        lax.psum_scatter(whole_up, "dp", scatter_dimension=0, tiled=True),
        lax.psum_scatter(whole_down, "dp", scatter_dimension=1, tiled=True),
        lax.psum_scatter(whole_gains, "dp", scatter_dimension=1, tiled=True),
        lax.psum_scatter(whole_shifts, "dp", scatter_dimension=1, tiled=True),
    )
    block_out = jnp.stack(results)[:, None]
    grad_in = jnp.stack(input_gradient_list)[:, None]
    return (block_out, grad_in, owned[0], owned[1], owned[2], owned[3], owned[4], owned[5])


def solution(mesh):
    in_specs = (
        P(None, "dp", "ctx", None),
        P(None, "dp"),
        P(),
        P(None, "dp", "tp"),
        P("tp", "dp"),
        P("dp", "tp"),
        P("tp", "dp"),
        P(None, "dp"),
        P(None, "dp"),
        P(None, "dp", "ctx", None),
    )
    out_specs = (
        P(None, "dp", "ctx", None),
        P(None, "dp", "ctx", None),
        P(None, "dp", "tp"),
        P("tp", "dp"),
        P("dp", "tp"),
        P("tp", "dp"),
        P(None, "dp"),
        P(None, "dp"),
    )
    return jax.shard_map(body, mesh=mesh, in_specs=in_specs, out_specs=out_specs, check_vma=False)
```

profile of v0, /device:TPU:0, one launch (start us, length us, event | category | flops | bytes accessed | tf_op | source)
XLA Modules:
  0.0 766.6 jit_solution(9417610063547408217)
XLA Ops:
  10.2 5.5 all_gather.20
  15.7 4.5 all_gather.21
  22.8 5.9 all_gather.49
  28.7 9.4 %all_gather.22 = bf16[3,768,192]{1,2,0:T(8,128)(2,1)S(1)} all-gather(bf16[3,384,192]{1,2,0:T(8,128)(2,1)S(1)} %copy-done.43), channel_id=1, replica_groups=mesh['dp'=2,'ctx'=4,'tp'=4] {'dp'}, dimensions={1}, use_global_device_ids=true | all-gather | bytes 1327104 | tf_op jit(solution)/shard_map/all_gather | solution.py:53
  39.8 19.5 %all-gather.3 = bf16[1,2048,192]{1,2,0:T(8,128)(2,1)S(1)} all-gather(bf16[1,512,192]{1,2,0:T(8,128)(2,1)S(1)} %get-tuple-element.187), channel_id=5, replica_groups=mesh['dp'=2,'ctx'=4,'tp'=4] {'ctx'}, dimensions={1}, use_global_device_ids=true | all-gather | bytes 983040 | tf_op jit(solution)/shard_map/all_gather | solution.py:113
  59.3 17.9 %all-gather.2 = bf16[1,2048,192]{1,2,0:T(8,128)(2,1)S(1)} all-gather(bf16[1,512,192]{1,2,0:T(8,128)(2,1)S(1)} %get-tuple-element.189), channel_id=4, replica_groups=mesh['dp'=2,'ctx'=4,'tp'=4] {'ctx'}, dimensions={1}, use_global_device_ids=true | all-gather | bytes 983040 | tf_op jit(solution)/shard_map/all_gather | solution.py:114
  78.2 17.1 %all-gather.1 = bf16[1,2048,192]{1,2,0:T(8,128)(2,1)S(1)} all-gather(bf16[1,512,192]{1,2,0:T(8,128)(2,1)S(1)} %get-tuple-element.184), channel_id=3, replica_groups=mesh['dp'=2,'ctx'=4,'tp'=4] {'ctx'}, dimensions={1}, use_global_device_ids=true | all-gather | bytes 983040 | tf_op jit(solution)/shard_map/all_gather | solution.py:113
  95.3 15.7 %all-gather = bf16[1,2048,192]{1,2,0:T(8,128)(2,1)S(1)} all-gather(bf16[1,512,192]{1,2,0:T(8,128)(2,1)S(1)} %get-tuple-element.186), channel_id=2, replica_groups=mesh['dp'=2,'ctx'=4,'tp'=4] {'ctx'}, dimensions={1}, use_global_device_ids=true | all-gather | bytes 983040 | tf_op jit(solution)/shard_map/all_gather | solution.py:114
  121.7 3.6 fusion.65
  140.2 68.0 %all-reduce.14.cloned.1.call-done = (f32[512,768]{1,0:T(8,128)}, f32[512,768]{1,0:T(8,128)}) async-done(((f32[512,768]{1,0:T(8,128)}, f32[512,768]{1,0:T(8,128)}), (f32[512,768]{1,0:T(8,128)}, f32[512,768]{1,0:T(8,128)})) %all-reduce.14.cloned.1.call-update) | async-done | bytes 3145744 | tf_op jit(solution)/shard_map/psum | solution.py:137
  211.8 3.9 fusion.114
  217.8 3.6 fusion.56
  227.0 68.7 %all-reduce.12.cloned.1.call-done = (f32[512,768]{1,0:T(8,128)}, f32[512,768]{1,0:T(8,128)}) async-done(((f32[512,768]{1,0:T(8,128)}, f32[512,768]{1,0:T(8,128)}), (f32[512,768]{1,0:T(8,128)}, f32[512,768]{1,0:T(8,128)})) %all-reduce.12.cloned.1.call-update) | async-done | bytes 3145744 | tf_op jit(solution)/shard_map/psum | solution.py:158
  295.7 3.8 multiply_reduce_fusion.3
  303.7 7.9 %fusion.6 = f32[3,64,2048]{2,1,0:T(8,128)} fusion(bf16[512,3,64]{0,2,1:T(8,128)(2,1)S(1)} %bitcast.237, f32[3,512,2048]{2,1,0:T(8,128)} %copy-done, f32[3,512]{1,0:T(4,128)S(1)} %log_add_fusion.1), kind=kOutput, calls=%fused_computation.17 | convolution fusion | flops 408944640 | bytes 14358528 | tf_op jit(solution)/shard_map/while/body/eval_jaxpr/hqk,qhd->khd/dot_general | solution.py:191
  313.8 8.2 %fusion.4 = f32[3,64,2048]{2,1,0:T(8,128)} fusion(bf16[512,3,64]{0,2,1:T(8,128)(2,1)S(1)} %bitcast.239, f32[3,512,2048]{2,1,0:T(8,128)} %copy-done.1, f32[3,512]{1,0:T(4,128)S(1)} %log_add_fusion), kind=kOutput, calls=%fused_computation.16 | convolution fusion | flops 408944640 | bytes 14358528 | tf_op jit(solution)/shard_map/while/body/eval_jaxpr/hqk,qhd->khd/dot_general | solution.py:191
  322.9 6.6 multiply_reduce_fusion
  329.5 6.5 multiply_convert_fusion
  339.9 6.6 multiply_reduce_fusion.1
  346.6 6.4 multiply_convert_fusion.1
  356.6 4.1 fusion.112
  360.7 3.9 fusion.111
  364.6 5.6 fusion.63
  374.0 10.4 %reduce-scatter.21.cloned.1.call-done = f32[512,192]{0,1:T(8,128)} async-done(((f32[2048,192]{0,1:T(8,128)}), f32[512,192]{0,1:T(8,128)}) %reduce-scatter.21.cloned.1.call-update) | async-done | bytes 393232 | tf_op jit(solution)/shard_map/reduce_scatter | solution.py:204
  385.4 35.6 %reduce-scatter.19.cloned.1.call-done = f32[512,192]{0,1:T(8,128)} async-done(((f32[2048,192]{0,1:T(8,128)}), f32[512,192]{0,1:T(8,128)}) %reduce-scatter.19.cloned.1.call-update) | async-done | bytes 393232 | tf_op jit(solution)/shard_map/reduce_scatter | solution.py:201
  426.0 31.6 %reduce-scatter.15.cloned.1.call-done = f32[512,192]{0,1:T(8,128)} async-done(((f32[2048,192]{0,1:T(8,128)}), f32[512,192]{0,1:T(8,128)}) %reduce-scatter.15.cloned.1.call-update) | async-done | bytes 393232 | tf_op jit(solution)/shard_map/reduce_scatter | solution.py:201
  459.3 3.3 convolution_bitcast_fusion.1
  483.8 97.4 %all-reduce.10.cloned.1.call-done = (f32[512,768]{1,0:T(8,128)}, f32[512,768]{1,0:T(8,128)}, f32[512,768]{1,0:T(8,128)}, f32[512,768]{1,0:T(8,128)}) async-done(((f32[512,768]{1,0:T(8,128)}, f32[512,768]{1,0:T(8,128)}, f32[512,768]{1,0:T(8,128)}, f32[512,768]{1,0:T(8,128)}), (f32[512,768]{1,0:T(8,128)}, f32[512,768]{1,0:T(8,128)}, f32[512,768]{1,0:T(8,128)}, ...) | async-done | bytes 6291472 | tf_op jit(solution)/shard_map/psum | solution.py:146
  595.7 5.8 reduce-scatter.33.cloned.1.call-done
  602.5 15.0 %reduce-scatter.31.cloned.1.call-done = f32[384,2]{1,0:T(8,128)} async-done(((f32[768,2]{1,0:T(8,128)}), f32[384,2]{1,0:T(8,128)}) %reduce-scatter.31.cloned.1.call-update) | async-done | bytes 3088
  618.5 12.6 %all-reduce.3 = (f32[2,384]{1,0:T(2,128)}, f32[2,384]{1,0:T(2,128)}) all-reduce(f32[2,384]{1,0:T(2,128)S(1)} %copy.25, f32[2,384]{1,0:T(2,128)S(1)} %copy.27), channel_id=1, replica_groups=mesh['dp'=2,'ctx'=4,'tp'=4] {'ctx'}, use_global_device_ids=true, to_apply=%region_48.49 | all-reduce | flops 1536 | bytes 12288 | tf_op jit(solution)/shard_map/psum | solution.py:237
  631.1 122.6 %all-reduce.16.cloned.1.call-done = (f32[3,384,192]{1,2,0:T(8,128)}, f32[192,384]{1,0:T(8,128)}, f32[384,768]{1,0:T(8,128)}, f32[768,384]{1,0:T(8,128)}) async-done(((f32[3,384,192]{1,2,0:T(8,128)}, f32[192,384]{1,0:T(8,128)}, f32[384,768]{1,0:T(8,128)}, f32[768,384]{1,0:T(8,128)}), (f32[3,384,192]{1,2,0:T(8,128)}, f32[192,384]{1,0:T(8,128)}, f32[384,768]{1,0:T(8,128)}, ...) | async-done | bytes 3538960 | tf_op jit(solution)/shard_map/psum | solution.py:237
  (305 shorter events, 112.2 us)
Async XLA Ops:
  8.0 200.2 %all-reduce.14.cloned.1.call-start = ((), (), s32[]{:S(2)}) async-start(), calls=%async_computation.24 | async-start | bytes 6291456 | tf_op jit(solution)/shard_map/psum | solution.py:137
  20.2 56.9 %copy-start.73 = (f32[768]{0:T(1024)}, f32[768]{0:T(1024)S(1)}, u32[]{:S(2)}) copy-start(f32[768]{0:T(1024)S(1)} %get-tuple-element.159) | copy-start | bytes 9220
  20.3 195.5 %copy-start.67 = (f32[768]{0:T(1024)}, f32[768]{0:T(1024)S(1)}, u32[]{:S(2)}) copy-start(f32[768]{0:T(1024)S(1)} %get-tuple-element.158) | copy-start | bytes 9220
  22.0 16.1 %copy-start.54 = (f32[512]{0:T(512)}, f32[512]{0:T(512)S(1)}, u32[]{:S(2)}) copy-start(f32[512]{0:T(512)S(1)} %broadcast_multiply_fusion.9) | copy-start | bytes 6148
  22.7 54.5 %copy-start.60 = (f32[512]{0:T(512)}, f32[512]{0:T(512)S(1)}, u32[]{:S(2)}) copy-start(f32[512]{0:T(512)S(1)} %add_rsqrt_fusion.3) | copy-start | bytes 6148
  22.7 16.3 %copy-start.62 = (f32[512]{0:T(512)}, f32[512]{0:T(512)S(1)}, u32[]{:S(2)}) copy-start(f32[512]{0:T(512)S(1)} %add_rsqrt_fusion.1) | copy-start | bytes 6148
  38.1 39.1 %copy-start.32 = (bf16[3,768,192]{1,2,0:T(8,128)(2,1)}, bf16[3,768,192]{1,2,0:T(8,128)(2,1)S(1)}, u32[]{:S(2)}) copy-start(bf16[3,768,192]{1,2,0:T(8,128)(2,1)S(1)} %all_gather.22) | copy-start | bytes 2654212
  59.3 67.6 %copy-start.17 = (bf16[1,2048,192]{1,2,0:T(8,128)(2,1)}, bf16[1,2048,192]{1,2,0:T(8,128)(2,1)S(1)}, u32[]{:S(2)}) copy-start(bf16[1,2048,192]{1,2,0:T(8,128)(2,1)S(1)} %all-gather.3) | copy-start | bytes 2359300
  77.2 54.3 %copy-start.16 = (bf16[1,2048,192]{1,2,0:T(8,128)(2,1)}, bf16[1,2048,192]{1,2,0:T(8,128)(2,1)S(1)}, u32[]{:S(2)}) copy-start(bf16[1,2048,192]{1,2,0:T(8,128)(2,1)S(1)} %all-gather.2) | copy-start | bytes 2359300
  78.2 36.3 %copy-start.39 = (bf16[1,512,192]{1,2,0:T(8,128)(2,1)}, bf16[1,512,192]{1,2,0:T(8,128)(2,1)S(1)}, u32[]{:S(2)}) copy-start(bf16[1,512,192]{1,2,0:T(8,128)(2,1)S(1)} %get-tuple-element.185) | copy-start | bytes 589828
  95.3 21.9 %copy-start.19 = (bf16[1,2048,192]{1,2,0:T(8,128)(2,1)}, bf16[1,2048,192]{1,2,0:T(8,128)(2,1)S(1)}, u32[]{:S(2)}) copy-start(bf16[1,2048,192]{1,2,0:T(8,128)(2,1)S(1)} %all-gather.1) | copy-start | bytes 2359300
  138.8 73.0 %all-gather.7.cloned.1.call-start = ((), (), s32[]{:S(2)}) async-start(), calls=%async_computation.10 | async-start | bytes 1769472 | tf_op jit(solution)/shard_map/all_gather | solution.py:55
  139.3 78.5 %all-gather.9.cloned.1.call-start = ((), (), s32[]{:S(2)}) async-start(), calls=%async_computation.11 | async-start | bytes 1769472 | tf_op jit(solution)/shard_map/all_gather | solution.py:56
  139.9 155.8 %all-reduce.12.cloned.1.call-start = ((), (), s32[]{:S(2)}) async-start(), calls=%async_computation.23 | async-start | bytes 6291456 | tf_op jit(solution)/shard_map/psum | solution.py:158
  210.6 88.9 %copy-start.56 = (f32[512]{0:T(512)}, f32[512]{0:T(512)S(1)}, u32[]{:S(2)}) copy-start(f32[512]{0:T(512)S(1)} %broadcast_multiply_fusion.10) | copy-start | bytes 6148
  211.8 87.8 %copy-start.58 = (f32[512]{0:T(512)}, f32[512]{0:T(512)S(1)}, u32[]{:S(2)}) copy-start(f32[512]{0:T(512)S(1)} %add_rsqrt_fusion) | copy-start | bytes 6148
  211.8 87.8 %copy-start.65 = (f32[512]{0:T(512)}, f32[512]{0:T(512)S(1)}, u32[]{:S(2)}) copy-start(f32[512]{0:T(512)S(1)} %add_rsqrt_fusion.2) | copy-start | bytes 6148
  226.9 146.0 %reduce-scatter.17.cloned.1.call-start = ((), (), s32[]{:S(2)}) async-start(), calls=%async_computation.13 | async-start | bytes 1966080 | tf_op jit(solution)/shard_map/reduce_scatter | solution.py:204
  311.6 72.8 %reduce-scatter.21.cloned.1.call-start = ((), (), s32[]{:S(2)}) async-start(), calls=%async_computation.15 | async-start | bytes 1966080 | tf_op jit(solution)/shard_map/reduce_scatter | solution.py:204
  322.0 99.0 %reduce-scatter.19.cloned.1.call-start = ((), (), s32[]{:S(2)}) async-start(), calls=%async_computation.14 | async-start | bytes 1966080 | tf_op jit(solution)/shard_map/reduce_scatter | solution.py:201
  339.0 118.6 %reduce-scatter.15.cloned.1.call-start = ((), (), s32[]{:S(2)}) async-start(), calls=%async_computation.12 | async-start | bytes 1966080 | tf_op jit(solution)/shard_map/reduce_scatter | solution.py:201
  356.3 224.9 %all-reduce.10.cloned.1.call-start = ((), (), s32[]{:S(2)}) async-start(), calls=%async_computation.22 | async-start | bytes 12582912 | tf_op jit(solution)/shard_map/psum | solution.py:146
  374.0 84.7 %copy-start.45 = (bf16[1,512,192]{1,2,0:T(8,128)(2,1)}, bf16[1,512,192]{1,2,0:T(8,128)(2,1)S(1)}, u32[]{:S(2)}) copy-start(bf16[1,512,192]{1,2,0:T(8,128)(2,1)S(1)} %convert_bitcast_fusion.6) | copy-start | bytes 589828
  385.4 40.5 %copy-start.47 = (bf16[1,512,192]{1,2,0:T(8,128)(2,1)}, bf16[1,512,192]{1,2,0:T(8,128)(2,1)S(1)}, u32[]{:S(2)}) copy-start(bf16[1,512,192]{1,2,0:T(8,128)(2,1)S(1)} %convert_bitcast_fusion.4) | copy-start | bytes 589828
  462.6 123.6 %reduce-scatter.25.cloned.1.call-start = ((), (), s32[]{:S(2)}) async-start(), calls=%async_computation.17 | async-start | bytes 884736 | tf_op jit(solution)/shard_map/reduce_scatter | solution.py:242
  466.6 119.7 %reduce-scatter.27.cloned.1.call-start = ((), (), s32[]{:S(2)}) async-start(), calls=%async_computation.18 | async-start | bytes 3538944 | tf_op jit(solution)/shard_map/reduce_scatter | solution.py:243
  472.3 114.0 %reduce-scatter.29.cloned.1.call-start = ((), (), s32[]{:S(2)}) async-start(), calls=%async_computation.19 | async-start | bytes 3538944 | tf_op jit(solution)/shard_map/reduce_scatter | solution.py:244
  478.0 108.3 %reduce-scatter.23.cloned.1.call-start = ((), (), s32[]{:S(2)}) async-start(), calls=%async_computation.16 | async-start | bytes 2654208 | tf_op jit(solution)/shard_map/reduce_scatter | solution.py:241
  483.1 98.1 %copy-start.64 = (f32[512]{0:T(512)S(1)}, f32[512]{0:T(512)}, u32[]{:S(2)}) copy-start(f32[512]{0:T(512)} %copy-done.62) | copy-start | bytes 6148
  483.1 118.4 %reduce-scatter.33.cloned.1.call-start = ((), (), s32[]{:S(2)}) async-start(), calls=%async_computation.21 | async-start | bytes 589824
  585.1 32.4 %reduce-scatter.31.cloned.1.call-start = ((), (), s32[]{:S(2)}) async-start(), calls=%async_computation.20 | async-start | bytes 589824
  586.2 167.6 %all-reduce.16.cloned.1.call-start = ((), (), s32[]{:S(2)}) async-start(), calls=%async_computation.25 | async-start | bytes 7077888 | tf_op jit(solution)/shard_map/psum | solution.py:237
  (69 other events, 228.5 us)
Sparse Core Ops, SparseCore 0:
  138.9 69.2 all-reduce.13
  227.1 68.5 all-reduce.11
  462.7 118.4 all-reduce.9
Sparse Core Ops, SparseCore 1:
  140.8 23.4 all-gather.6
  165.7 22.6 all-gather.8
  311.7 35.5 reduce-scatter.16
  350.2 34.2 reduce-scatter.20
  386.7 34.2 reduce-scatter.18
  423.4 34.2 reduce-scatter.14
  466.7 14.0 reduce-scatter.24
  483.5 34.7 reduce-scatter.26
  520.3 34.7 reduce-scatter.28
  557.4 28.2 reduce-scatter.22
  588.3 13.1 reduce-scatter.32
  604.3 13.1 reduce-scatter.30
  620.0 133.7 all-reduce.15
where the time goes:
time: 775 us; the launch traced here: 767 us
  waiting for transfers between devices  457 us (59%)
  matrix products  110 us (14%)
  blocking collectives  108 us (14%)
  other arithmetic  46.1 us (6%)
  local copies, waits for them, and re-layouts  26.5 us (3%)
  between operations  17.2 us (2%)
    psum x1, waiting for transfers between devices, body(): lax.psum((acc_qkv, acc_out, acc_up, acc_down, acc_gains, acc_shifts), 'ctx')  123 us
    psum x1, waiting for transfers between devices, body(): mlp = lax.psum(mlp_part, 'tp')  97.4 us
    psum x1, waiting for transfers between devices, body(): second_norm_gradient = lax.psum(n2_back, 'tp')  68.7 us
    psum x1, waiting for transfers between devices, body(): attn = lax.psum(attn_part, 'tp')  68 us
    reduce_scatter x2, waiting for transfers between devices, body(): lax.psum_scatter(key_sum.reshape(seq_len, local_width), 'ctx', scatter_di...  67.2 us
    all_gather x2, blocking collectives, body(): lax.all_gather(qkv[1], 'ctx', axis=0, tiled=True)  36.6 us
    all_gather x2, blocking collectives, body(): lax.all_gather(qkv[2], 'ctx', axis=0, tiled=True)  33.6 us
    unnamed x178, local copies, waits for them, and re-layouts  24.3 us
  transfers between devices with their start and end apart: 16, of which 9 were waited for; matrix products, arithmetic and copies ran while one was open for 14% of the time, Pallas kernels for 0%

commit v1 on v0

--- a/solution.py
+++ b/solution.py
@@ -155,7 +155,7 @@
         d_up = (d_act * gelu_slope(up)).astype(jnp.bfloat16)
         grad_up = jnp.einsum("td,tf->df", h2, d_up, preferred_element_type=jnp.float32)
         n2_back = jnp.einsum("tf,df->td", d_up, up_full, preferred_element_type=jnp.float32)
-        second_norm_gradient = lax.psum(n2_back, "tp")
+        second_norm_gradient = jnp.sum(lax.all_gather(n2_back, "tp"), axis=0)
         middle_gradient = upstream_gradient + norm_backward(
             second_norm_gradient, normalized_second2, inverse_deviation2, norm_gains[1]
         )

time: 775 us -> 802 us (1.035)
  other arithmetic: 46.1 us -> 65 us
  starting transfers between devices: 1.62 us -> 12.6 us
    all_gather x0 -> x2, waiting for transfers between devices: none -> 70.5 us  [body(): second_norm_gradient = jnp.sum(lax.all_gather(n2_back, 'tp'), axis=0)]
    psum x1 -> x0, waiting for transfers between devices: 68.7 us -> none  [body(): second_norm_gradient = lax.psum(n2_back, 'tp')]
    reduce_sum x0 -> x4, other arithmetic: none -> 15.7 us  [the longest x2 9.03 us: body(): second_norm_gradient = jnp.sum(lax.all_gather(n2_back, 'tp'), axis=0)]
    all_gather x0 -> x2, starting transfers between devices: none -> 11.5 us  [body(): second_norm_gradient = jnp.sum(lax.all_gather(n2_back, 'tp'), axis=0)]
    unnamed x18 -> x19, waiting for transfers between devices: 22.5 us -> 23.5 us
    unnamed x178 -> x172, local copies, waits for them, and re-layouts: 24.3 us -> 24.1 us
  transfers between devices with their start and end apart: 16 -> 17, of which waited for: 9 -> 11; matrix products, arithmetic and copies ran while one was open for 14% -> 15% of each run, Pallas kernels for 0% -> 0%
where the time goes in v1:
time: 802 us; the launch traced here: 794 us
  waiting for transfers between devices  456 us (57%)
  matrix products  109 us (14%)
  blocking collectives  108 us (13%)
  other arithmetic  65 us (8%)
  local copies, waits for them, and re-layouts  26.3 us (3%)
  between operations  17.2 us (2%)
  starting transfers between devices  12.6 us (2%)
    psum x1, waiting for transfers between devices, body(): lax.psum((acc_qkv, acc_out, acc_up, acc_down, acc_gains, acc_shifts), 'ctx')  123 us
    psum x1, waiting for transfers between devices, body(): mlp = lax.psum(mlp_part, 'tp')  91.7 us
    all_gather x2, waiting for transfers between devices, body(): second_norm_gradient = jnp.sum(lax.all_gather(n2_back, 'tp'), axis=0)  70.5 us
    psum x1, waiting for transfers between devices, body(): attn = lax.psum(attn_part, 'tp')  68.2 us
    reduce_scatter x2, waiting for transfers between devices, body(): lax.psum_scatter(key_sum.reshape(seq_len, local_width), 'ctx', scatter_di...  67.2 us
    all_gather x2, blocking collectives, body(): lax.all_gather(qkv[1], 'ctx', axis=0, tiled=True)  36.6 us
    all_gather x2, blocking collectives, body(): lax.all_gather(qkv[2], 'ctx', axis=0, tiled=True)  33.6 us
    unnamed x172, local copies, waits for them, and re-layouts  24.1 us
  transfers between devices with their start and end apart: 17, of which 11 were waited for; matrix products, arithmetic and copies ran while one was open for 15% of the time, Pallas kernels for 0%

profile of v1, /device:TPU:0, one launch (start us, length us, event | category | flops | bytes accessed | tf_op | source)
XLA Modules:
  0.0 793.8 jit_solution(18335861244914604201)
XLA Ops:
  10.2 5.5 all_gather.56
  15.7 4.5 all_gather.57
  22.8 5.9 all_gather.61
  28.8 9.4 %all_gather.58 = bf16[3,768,192]{1,2,0:T(8,128)(2,1)S(1)} all-gather(bf16[3,384,192]{1,2,0:T(8,128)(2,1)S(1)} %copy-done.42), channel_id=1, replica_groups=mesh['dp'=2,'ctx'=4,'tp'=4] {'dp'}, dimensions={1}, use_global_device_ids=true | all-gather | bytes 1327104 | tf_op jit(solution)/shard_map/all_gather | solution.py:53
  39.8 19.5 %all-gather.3 = bf16[1,2048,192]{1,2,0:T(8,128)(2,1)S(1)} all-gather(bf16[1,512,192]{1,2,0:T(8,128)(2,1)S(1)} %get-tuple-element.183), channel_id=5, replica_groups=mesh['dp'=2,'ctx'=4,'tp'=4] {'ctx'}, dimensions={1}, use_global_device_ids=true | all-gather | bytes 983040 | tf_op jit(solution)/shard_map/all_gather | solution.py:113
  59.3 17.8 %all-gather.2 = bf16[1,2048,192]{1,2,0:T(8,128)(2,1)S(1)} all-gather(bf16[1,512,192]{1,2,0:T(8,128)(2,1)S(1)} %get-tuple-element.185), channel_id=4, replica_groups=mesh['dp'=2,'ctx'=4,'tp'=4] {'ctx'}, dimensions={1}, use_global_device_ids=true | all-gather | bytes 983040 | tf_op jit(solution)/shard_map/all_gather | solution.py:114
  78.2 17.1 %all-gather.1 = bf16[1,2048,192]{1,2,0:T(8,128)(2,1)S(1)} all-gather(bf16[1,512,192]{1,2,0:T(8,128)(2,1)S(1)} %get-tuple-element.180), channel_id=3, replica_groups=mesh['dp'=2,'ctx'=4,'tp'=4] {'ctx'}, dimensions={1}, use_global_device_ids=true | all-gather | bytes 983040 | tf_op jit(solution)/shard_map/all_gather | solution.py:113
  95.3 15.7 %all-gather = bf16[1,2048,192]{1,2,0:T(8,128)(2,1)S(1)} all-gather(bf16[1,512,192]{1,2,0:T(8,128)(2,1)S(1)} %get-tuple-element.182), channel_id=2, replica_groups=mesh['dp'=2,'ctx'=4,'tp'=4] {'ctx'}, dimensions={1}, use_global_device_ids=true | all-gather | bytes 983040 | tf_op jit(solution)/shard_map/all_gather | solution.py:114
  139.8 68.2 %all-reduce.10.cloned.1.call-done = (f32[512,768]{1,0:T(8,128)}, f32[512,768]{1,0:T(8,128)}) async-done(((f32[512,768]{1,0:T(8,128)}, f32[512,768]{1,0:T(8,128)}), (f32[512,768]{1,0:T(8,128)}, f32[512,768]{1,0:T(8,128)})) %all-reduce.10.cloned.1.call-update) | async-done | bytes 3145744 | tf_op jit(solution)/shard_map/psum | solution.py:137
  221.6 11.5 %all-gather.15.cloned.1.call-start = ((), (), s32[]{:S(2)}) async-start(), calls=%async_computation.16 | async-start | bytes 7864320 | tf_op jit(solution)/shard_map/all_gather | solution.py:158
  241.7 26.4 %all-gather.17.cloned.1.call-done = f32[2048,768]{1,0:T(8,128)} async-done(((f32[512,768]{1,0:T(8,128)}), f32[2048,768]{1,0:T(8,128)}) %all-gather.17.cloned.1.call-update) | async-done | bytes 6291472 | tf_op jit(solution)/shard_map/all_gather | solution.py:158
  268.2 4.5 reduce_sum.310
  272.7 44.0 %all-gather.15.cloned.1.call-done = f32[2048,768]{1,0:T(8,128)} async-done(((f32[512,768]{1,0:T(8,128)}), f32[2048,768]{1,0:T(8,128)}) %all-gather.15.cloned.1.call-update) | async-done | bytes 6291472 | tf_op jit(solution)/shard_map/all_gather | solution.py:158
  316.7 4.5 reduce_sum.304
  321.2 3.8 multiply_reduce_fusion.3
  329.2 8.0 %fusion.6 = f32[3,64,2048]{2,1,0:T(8,128)} fusion(bf16[512,3,64]{0,2,1:T(8,128)(2,1)S(1)} %bitcast.241, f32[3,512,2048]{2,1,0:T(8,128)} %copy-done, f32[3,512]{1,0:T(4,128)S(1)} %log_add_fusion.1), kind=kOutput, calls=%fused_computation.17 | convolution fusion | flops 408944640 | bytes 14358528 | tf_op jit(solution)/shard_map/while/body/eval_jaxpr/hqk,qhd->khd/dot_general | solution.py:191
  339.0 8.2 %fusion.4 = f32[3,64,2048]{2,1,0:T(8,128)} fusion(bf16[512,3,64]{0,2,1:T(8,128)(2,1)S(1)} %bitcast.243, f32[3,512,2048]{2,1,0:T(8,128)} %copy-done.1, f32[3,512]{1,0:T(4,128)S(1)} %log_add_fusion), kind=kOutput, calls=%fused_computation.16 | convolution fusion | flops 408944640 | bytes 14358528 | tf_op jit(solution)/shard_map/while/body/eval_jaxpr/hqk,qhd->khd/dot_general | solution.py:191
  348.1 6.6 multiply_reduce_fusion
  354.7 6.5 multiply_convert_fusion
  365.3 6.6 multiply_reduce_fusion.1
  371.9 6.4 multiply_convert_fusion.1
  381.9 4.1 fusion.112
  386.0 3.8 fusion.111
  389.8 5.6 fusion.63
  399.2 10.6 %reduce-scatter.21.cloned.1.call-done = f32[512,192]{0,1:T(8,128)} async-done(((f32[2048,192]{0,1:T(8,128)}), f32[512,192]{0,1:T(8,128)}) %reduce-scatter.21.cloned.1.call-update) | async-done | bytes 393232 | tf_op jit(solution)/shard_map/reduce_scatter | solution.py:204
  410.9 35.6 %reduce-scatter.19.cloned.1.call-done = f32[512,192]{0,1:T(8,128)} async-done(((f32[2048,192]{0,1:T(8,128)}), f32[512,192]{0,1:T(8,128)}) %reduce-scatter.19.cloned.1.call-update) | async-done | bytes 393232 | tf_op jit(solution)/shard_map/reduce_scatter | solution.py:201
  451.4 31.6 %reduce-scatter.15.cloned.1.call-done = f32[512,192]{0,1:T(8,128)} async-done(((f32[2048,192]{0,1:T(8,128)}), f32[512,192]{0,1:T(8,128)}) %reduce-scatter.15.cloned.1.call-update) | async-done | bytes 393232 | tf_op jit(solution)/shard_map/reduce_scatter | solution.py:201
  514.9 91.7 %all-reduce.8.cloned.1.call-done = (f32[512,768]{1,0:T(8,128)}, f32[512,768]{1,0:T(8,128)}, f32[512,768]{1,0:T(8,128)}, f32[512,768]{1,0:T(8,128)}) async-done(((f32[512,768]{1,0:T(8,128)}, f32[512,768]{1,0:T(8,128)}, f32[512,768]{1,0:T(8,128)}, f32[512,768]{1,0:T(8,128)}), (f32[512,768]{1,0:T(8,128)}, f32[512,768]{1,0:T(8,128)}, f32[512,768]{1,0:T(8,128)}, ...) | async-done | bytes 6291472 | tf_op jit(solution)/shard_map/psum | solution.py:146
  621.5 7.2 reduce-scatter.33.cloned.1.call-done
  629.8 15.0 %reduce-scatter.31.cloned.1.call-done = f32[384,2]{1,0:T(8,128)} async-done(((f32[768,2]{1,0:T(8,128)}), f32[384,2]{1,0:T(8,128)}) %reduce-scatter.31.cloned.1.call-update) | async-done | bytes 3088
  645.8 12.6 %all-reduce.2 = (f32[2,384]{1,0:T(2,128)}, f32[2,384]{1,0:T(2,128)}) all-reduce(f32[2,384]{1,0:T(2,128)S(1)} %copy.25, f32[2,384]{1,0:T(2,128)S(1)} %copy.27), channel_id=1, replica_groups=mesh['dp'=2,'ctx'=4,'tp'=4] {'ctx'}, use_global_device_ids=true, to_apply=%region_48.49 | all-reduce | flops 1536 | bytes 12288 | tf_op jit(solution)/shard_map/psum | solution.py:237
  658.4 122.6 %all-reduce.12.cloned.1.call-done = (f32[3,384,192]{1,2,0:T(8,128)}, f32[192,384]{1,0:T(8,128)}, f32[384,768]{1,0:T(8,128)}, f32[768,384]{1,0:T(8,128)}) async-done(((f32[3,384,192]{1,2,0:T(8,128)}, f32[192,384]{1,0:T(8,128)}, f32[384,768]{1,0:T(8,128)}, f32[768,384]{1,0:T(8,128)}), (f32[3,384,192]{1,2,0:T(8,128)}, f32[192,384]{1,0:T(8,128)}, f32[384,768]{1,0:T(8,128)}, ...) | async-done | bytes 3538960 | tf_op jit(solution)/shard_map/psum | solution.py:237
  (304 shorter events, 135.6 us)
Async XLA Ops:
  8.0 200.0 %all-reduce.10.cloned.1.call-start = ((), (), s32[]{:S(2)}) async-start(), calls=%async_computation.25 | async-start | bytes 6291456 | tf_op jit(solution)/shard_map/psum | solution.py:137
  15.7 61.5 %copy-start.53 = (f32[768]{0:T(1024)}, f32[768]{0:T(1024)S(1)}, u32[]{:S(2)}) copy-start(f32[768]{0:T(1024)S(1)} %get-tuple-element.155) | copy-start | bytes 9220
  20.3 56.9 %copy-start.70 = (f32[768]{0:T(1024)}, f32[768]{0:T(1024)S(1)}, u32[]{:S(2)}) copy-start(f32[768]{0:T(1024)S(1)} %get-tuple-element.157) | copy-start | bytes 9220
  20.3 214.6 %copy-start.66 = (f32[768]{0:T(1024)}, f32[768]{0:T(1024)S(1)}, u32[]{:S(2)}) copy-start(f32[768]{0:T(1024)S(1)} %get-tuple-element.156) | copy-start | bytes 9220
  22.0 55.1 %copy-start.55 = (f32[512]{0:T(512)}, f32[512]{0:T(512)S(1)}, u32[]{:S(2)}) copy-start(f32[512]{0:T(512)S(1)} %broadcast_multiply_fusion.11) | copy-start | bytes 6148
  22.7 54.5 %copy-start.59 = (f32[512]{0:T(512)}, f32[512]{0:T(512)S(1)}, u32[]{:S(2)}) copy-start(f32[512]{0:T(512)S(1)} %add_rsqrt_fusion.3) | copy-start | bytes 6148
  22.7 16.3 %copy-start.61 = (f32[512]{0:T(512)}, f32[512]{0:T(512)S(1)}, u32[]{:S(2)}) copy-start(f32[512]{0:T(512)S(1)} %add_rsqrt_fusion.1) | copy-start | bytes 6148
  38.1 39.1 %copy-start.31 = (bf16[3,768,192]{1,2,0:T(8,128)(2,1)}, bf16[3,768,192]{1,2,0:T(8,128)(2,1)S(1)}, u32[]{:S(2)}) copy-start(bf16[3,768,192]{1,2,0:T(8,128)(2,1)S(1)} %all_gather.58) | copy-start | bytes 2654212
  59.3 67.3 %copy-start.17 = (bf16[1,2048,192]{1,2,0:T(8,128)(2,1)}, bf16[1,2048,192]{1,2,0:T(8,128)(2,1)S(1)}, u32[]{:S(2)}) copy-start(bf16[1,2048,192]{1,2,0:T(8,128)(2,1)S(1)} %all-gather.3) | copy-start | bytes 2359300
  77.2 54.1 %copy-start.16 = (bf16[1,2048,192]{1,2,0:T(8,128)(2,1)}, bf16[1,2048,192]{1,2,0:T(8,128)(2,1)S(1)}, u32[]{:S(2)}) copy-start(bf16[1,2048,192]{1,2,0:T(8,128)(2,1)S(1)} %all-gather.2) | copy-start | bytes 2359300
  78.2 36.3 %copy-start.38 = (bf16[1,512,192]{1,2,0:T(8,128)(2,1)}, bf16[1,512,192]{1,2,0:T(8,128)(2,1)S(1)}, u32[]{:S(2)}) copy-start(bf16[1,512,192]{1,2,0:T(8,128)(2,1)S(1)} %get-tuple-element.181) | copy-start | bytes 589828
  95.3 21.9 %copy-start.19 = (bf16[1,2048,192]{1,2,0:T(8,128)(2,1)}, bf16[1,2048,192]{1,2,0:T(8,128)(2,1)S(1)}, u32[]{:S(2)}) copy-start(bf16[1,2048,192]{1,2,0:T(8,128)(2,1)S(1)} %all-gather.1) | copy-start | bytes 2359300
  138.6 73.2 %all-gather.11.cloned.1.call-start = ((), (), s32[]{:S(2)}) async-start(), calls=%async_computation.10 | async-start | bytes 1769472 | tf_op jit(solution)/shard_map/all_gather | solution.py:55
  139.2 76.0 %all-gather.13.cloned.1.call-start = ((), (), s32[]{:S(2)}) async-start(), calls=%async_computation.11 | async-start | bytes 1769472 | tf_op jit(solution)/shard_map/all_gather | solution.py:56
  139.8 128.4 %all-gather.17.cloned.1.call-start = ((), (), s32[]{:S(2)}) async-start(), calls=%async_computation.17 | async-start | bytes 7864320 | tf_op jit(solution)/shard_map/all_gather | solution.py:158
  221.6 95.1 %all-gather.15.cloned.1.call-start = ((), (), s32[]{:S(2)}) async-start(), calls=%async_computation.16 | async-start | bytes 7864320 | tf_op jit(solution)/shard_map/all_gather | solution.py:158
  234.9 90.1 %copy-start.64 = (f32[512]{0:T(512)}, f32[512]{0:T(512)S(1)}, u32[]{:S(2)}) copy-start(f32[512]{0:T(512)S(1)} %add_rsqrt_fusion.2) | copy-start | bytes 6148
  241.7 156.5 %reduce-scatter.17.cloned.1.call-start = ((), (), s32[]{:S(2)}) async-start(), calls=%async_computation.13 | async-start | bytes 1966080 | tf_op jit(solution)/shard_map/reduce_scatter | solution.py:204
  337.1 72.7 %reduce-scatter.21.cloned.1.call-start = ((), (), s32[]{:S(2)}) async-start(), calls=%async_computation.15 | async-start | bytes 1966080 | tf_op jit(solution)/shard_map/reduce_scatter | solution.py:204
  347.2 99.2 %reduce-scatter.19.cloned.1.call-start = ((), (), s32[]{:S(2)}) async-start(), calls=%async_computation.14 | async-start | bytes 1966080 | tf_op jit(solution)/shard_map/reduce_scatter | solution.py:201
  364.4 118.6 %reduce-scatter.15.cloned.1.call-start = ((), (), s32[]{:S(2)}) async-start(), calls=%async_computation.12 | async-start | bytes 1966080 | tf_op jit(solution)/shard_map/reduce_scatter | solution.py:201
  381.6 225.0 %all-reduce.8.cloned.1.call-start = ((), (), s32[]{:S(2)}) async-start(), calls=%async_computation.24 | async-start | bytes 12582912 | tf_op jit(solution)/shard_map/psum | solution.py:146
  399.2 84.8 %copy-start.44 = (bf16[1,512,192]{1,2,0:T(8,128)(2,1)}, bf16[1,512,192]{1,2,0:T(8,128)(2,1)S(1)}, u32[]{:S(2)}) copy-start(bf16[1,512,192]{1,2,0:T(8,128)(2,1)S(1)} %convert_bitcast_fusion.6) | copy-start | bytes 589828
  410.8 40.5 %copy-start.46 = (bf16[1,512,192]{1,2,0:T(8,128)(2,1)}, bf16[1,512,192]{1,2,0:T(8,128)(2,1)S(1)}, u32[]{:S(2)}) copy-start(bf16[1,512,192]{1,2,0:T(8,128)(2,1)S(1)} %convert_bitcast_fusion.4) | copy-start | bytes 589828
  488.0 123.6 %reduce-scatter.27.cloned.1.call-start = ((), (), s32[]{:S(2)}) async-start(), calls=%async_computation.20 | async-start | bytes 3538944 | tf_op jit(solution)/shard_map/reduce_scatter | solution.py:243
  493.8 117.8 %reduce-scatter.29.cloned.1.call-start = ((), (), s32[]{:S(2)}) async-start(), calls=%async_computation.21 | async-start | bytes 3538944 | tf_op jit(solution)/shard_map/reduce_scatter | solution.py:244
  499.5 112.2 %reduce-scatter.25.cloned.1.call-start = ((), (), s32[]{:S(2)}) async-start(), calls=%async_computation.19 | async-start | bytes 884736 | tf_op jit(solution)/shard_map/reduce_scatter | solution.py:242
  503.6 109.4 %reduce-scatter.23.cloned.1.call-start = ((), (), s32[]{:S(2)}) async-start(), calls=%async_computation.18 | async-start | bytes 2654208 | tf_op jit(solution)/shard_map/reduce_scatter | solution.py:241
  508.1 120.6 %reduce-scatter.33.cloned.1.call-start = ((), (), s32[]{:S(2)}) async-start(), calls=%async_computation.23 | async-start | bytes 589824
  511.6 95.0 %copy-start.63 = (f32[512]{0:T(512)S(1)}, f32[512]{0:T(512)}, u32[]{:S(2)}) copy-start(f32[512]{0:T(512)} %copy-done.61) | copy-start | bytes 6148
  610.5 34.2 %reduce-scatter.31.cloned.1.call-start = ((), (), s32[]{:S(2)}) async-start(), calls=%async_computation.22 | async-start | bytes 589824
  611.5 169.5 %all-reduce.12.cloned.1.call-start = ((), (), s32[]{:S(2)}) async-start(), calls=%async_computation.26 | async-start | bytes 7077888 | tf_op jit(solution)/shard_map/psum | solution.py:237
  (67 other events, 239.8 us)
Sparse Core Ops, SparseCore 0:
  138.7 69.2 all-reduce.9
  221.7 46.4 all-gather.16
  270.3 46.3 all-gather.14
  488.1 118.4 all-reduce.7
Sparse Core Ops, SparseCore 1:
  140.6 23.4 all-gather.10
  165.5 22.6 all-gather.12
  337.2 35.4 reduce-scatter.16
  375.6 34.2 reduce-scatter.20
  412.1 34.2 reduce-scatter.18
  448.7 34.2 reduce-scatter.14
  493.9 33.5 reduce-scatter.26
  529.6 34.7 reduce-scatter.28
  567.0 15.3 reduce-scatter.24
  584.7 28.2 reduce-scatter.22
  615.6 13.1 reduce-scatter.32
  631.6 13.1 reduce-scatter.30
  647.3 133.7 all-reduce.11
